TPU v7x, 32 devices: a whole 2x2x4 slice. The times are simulated.
32 devices in a mesh: dp: 16 (over z, x, core), seq: 2 (over y).
Axes of the slice: x: 2, y: 2, z: 4, core: 2. Of those that a mesh axis runs over, the one named last changes fastest.
Arguments:
- tokens: bfloat16 [16, 1152, 1024], P('dp', 'seq'), may hold values from -6 to 6
- w_qkv: bfloat16 [1024, 3072], P('dp'), may hold values from -0.1875 to 0.1875
- w_out: bfloat16 [1024, 1024], P('dp'), may hold values from -1 to 1
- w_up: bfloat16 [1024, 4096], P('dp'), may hold values from -0.1875 to 0.1875
- w_down: bfloat16 [4096, 1024], P('dp'), may hold values from -0.09375 to 0.09375
- gains: bfloat16 [1024, 2], P('dp'), may hold values from 0.5 to 1.5
- biases: bfloat16 [1024, 6], P('dp'), may hold values from -1.1953125 to 1.1953125
- up_bias: bfloat16 [4096], P('dp'), may hold values from -1.1953125 to 1.1953125
- valid: int32 [16], P('dp'), may hold values from 577 to 1152
- cotangent: bfloat16 [16, 1152, 1024], P('dp', 'seq'), may hold values from -6 to 6
Outputs:
- out_tokens: bfloat16 [16, 1152, 1024], P('dp', 'seq')
- grad_tokens: float32 [16, 1152, 1024], P('dp', 'seq')
- grad_qkv: float32 [1024, 3072], P('dp')
- grad_out: float32 [1024, 1024], P('dp')
- grad_up: float32 [1024, 4096], P('dp')
- grad_down: float32 [4096, 1024], P('dp')
- grad_gains: float32 [1024, 2], P('dp')
- grad_biases: float32 [1024, 6], P('dp')
- grad_up_bias: float32 [4096], P('dp')
Inputs may be any that keep to these rules, and one draw needn't show every extreme that they name: valid counts of the images; keys at positions from valid on are padding.
All inputs are finite; a program needn't handle non-finite values.
Results may differ from a plain program's by a relative error of at most 0.019.
Values may be sent and summed in bfloat16 or wider, within the bound.
A program may use at most 256 MiB of HBM per device.

v0:
```python
import jax
import jax.numpy as jnp
from jax import lax
from jax.sharding import PartitionSpec as P

HD = 64
EPSILON = 1e-06
NEG_FILL = -1e30


def layer_norm(values, scales, offset):
    average = jnp.mean(values, axis=-1, keepdims=True)
    centered = values - average
    variance = jnp.mean(centered * centered, axis=-1, keepdims=True)
    return centered * lax.rsqrt(variance + EPSILON) * scales + offset


def exact_gelu(values):
    return jax.nn.gelu(values, approximate=False)


def split_heads(block):
    seq_len = block.shape[0]
    return block.reshape(seq_len, block.shape[1] // HD, HD)


def score_block(query_heads, key_heads, length):
    scores = jnp.einsum("qhd,khd->hqk", query_heads, key_heads, preferred_element_type=jnp.float32)
    scores = scores * HD ** (-0.5)
    allowed = jnp.arange(key_heads.shape[0], dtype=jnp.int32) < length
    return jnp.where(allowed[None, None, :], scores, NEG_FILL)


def attend_forward(packed):
    queries, keyset, values, length = packed
    query_heads = split_heads(queries)
    key_heads = split_heads(keyset)
    value_heads = split_heads(values)
    scores = score_block(query_heads, key_heads, length)
    row_max = jnp.max(scores, axis=-1, keepdims=True)
    exp_scores = jnp.exp(scores - row_max)
    row_total = jnp.sum(exp_scores, axis=-1, keepdims=True)
    probs = (exp_scores / row_total).astype(jnp.bfloat16)
    result = jnp.einsum("hqk,khd->qhd", probs, value_heads, preferred_element_type=jnp.float32)
    log_total = row_max[..., 0] + jnp.log(row_total[..., 0])
    return (result.reshape(queries.shape).astype(jnp.bfloat16), log_total)


def attend_backward(packed):
    queries, keyset, values, length, log_total, grad_result = packed
    query_heads = split_heads(queries)
    key_heads = split_heads(keyset)
    value_heads = split_heads(values)
    grad_heads = split_heads(grad_result)
    scores = score_block(query_heads, key_heads, length)
    probs = jnp.exp(scores - log_total[:, :, None])
    grad_probs = jnp.einsum(
        "qhd,khd->hqk", grad_heads, value_heads, preferred_element_type=jnp.float32
    )
    row_delta = jnp.sum(probs * grad_probs, axis=-1, keepdims=True)
    grad_scores = (probs * (grad_probs - row_delta)).astype(jnp.bfloat16)
    grad_query = jnp.einsum(
        "hqk,khd->qhd", grad_scores, key_heads, preferred_element_type=jnp.float32
    ) * HD ** (-0.5)
    grad_key = jnp.einsum(
        "hqk,qhd->khd", grad_scores, query_heads, preferred_element_type=jnp.float32
    ) * HD ** (-0.5)
    grad_value = jnp.einsum(
        "hqk,qhd->khd", probs.astype(jnp.bfloat16), grad_heads, preferred_element_type=jnp.float32
    )
    flat_shape = queries.shape
    return (
        grad_query.reshape(flat_shape).astype(jnp.bfloat16),
        grad_key.reshape(flat_shape).astype(jnp.bfloat16),
        grad_value.reshape(flat_shape).astype(jnp.bfloat16),
    )


def per_device(tokens, w_qkv, w_out, w_up, w_down, gains, biases, up_bias, valid, cotangent):
    full_qkv, full_out, full_up, full_down, full_gains, full_biases, full_upb = (
        lax.all_gather(w_qkv, "dp", axis=0, tiled=True),
        lax.all_gather(w_out, "dp", axis=0, tiled=True),
        lax.all_gather(w_up, "dp", axis=0, tiled=True),
        lax.all_gather(w_down, "dp", axis=0, tiled=True),
        lax.all_gather(gains, "dp", axis=0, tiled=True),
        lax.all_gather(biases, "dp", axis=0, tiled=True),
        lax.all_gather(up_bias, "dp", axis=0, tiled=True),
    )
    gain_cols = full_gains.astype(jnp.float32)
    bias_cols = full_biases.astype(jnp.float32)
    upb_float = full_upb.astype(jnp.float32)
    images, local_len, model_width = tokens.shape
    token_shape = (images, local_len, model_width)
    flat_tokens = tokens.reshape(-1, model_width).astype(jnp.float32)
    normed_one, pull_one = jax.vjp(layer_norm, flat_tokens, gain_cols[:, 0], bias_cols[:, 0])
    first = normed_one.astype(jnp.bfloat16)
    mixed = jnp.dot(first, full_qkv, preferred_element_type=jnp.float32)
    queries = (mixed[:, :model_width] + bias_cols[:, 1]).astype(jnp.bfloat16)
    keyset = mixed[:, model_width : 2 * model_width].astype(jnp.bfloat16)
    values = (mixed[:, 2 * model_width :] + bias_cols[:, 2]).astype(jnp.bfloat16)
    head_q, head_k, head_v = (
        lax.all_to_all(
            queries.reshape(token_shape), "seq", split_axis=2, concat_axis=1, tiled=True
        ),
        lax.all_to_all(keyset.reshape(token_shape), "seq", split_axis=2, concat_axis=1, tiled=True),
        lax.all_to_all(values.reshape(token_shape), "seq", split_axis=2, concat_axis=1, tiled=True),
    )
    attended, log_totals = lax.map(attend_forward, (head_q, head_k, head_v, valid))
    back_tokens = lax.all_to_all(attended, "seq", split_axis=1, concat_axis=2, tiled=True)
    merged = back_tokens.reshape(-1, model_width)
    branch = jnp.dot(merged, full_out, preferred_element_type=jnp.float32) + bias_cols[:, 3]
    residual = flat_tokens + branch
    normed_two, pull_two = jax.vjp(layer_norm, residual, gain_cols[:, 1], bias_cols[:, 4])
    second = normed_two.astype(jnp.bfloat16)
    upward = jnp.dot(second, full_up, preferred_element_type=jnp.float32) + upb_float
    activated_float, pull_gelu = jax.vjp(exact_gelu, upward)
    activated = activated_float.astype(jnp.bfloat16)
    output = (
        residual
        + jnp.dot(activated, full_down, preferred_element_type=jnp.float32)
        + bias_cols[:, 5]
    )
    out_tokens = output.astype(jnp.bfloat16).reshape(token_shape)
    back_qkv, back_out, back_up, back_down = (full_qkv, full_out, full_up, full_down)
    grad_output = cotangent.reshape(-1, model_width)
    grad_down = jnp.dot(activated.T, grad_output, preferred_element_type=jnp.float32)
    grad_bias_down = jnp.sum(grad_output.astype(jnp.float32), axis=0)
    grad_act = jnp.dot(grad_output, back_down.T, preferred_element_type=jnp.float32)
    grad_upward = pull_gelu(grad_act)[0].astype(jnp.bfloat16)
    grad_up = jnp.dot(second.T, grad_upward, preferred_element_type=jnp.float32)
    grad_up_bias = jnp.sum(grad_upward.astype(jnp.float32), axis=0)
    grad_second = jnp.dot(grad_upward, back_up.T, preferred_element_type=jnp.float32)
    grad_resid_norm, grad_gain_two, grad_bias_two = pull_two(grad_second)
    grad_resid = grad_output.astype(jnp.float32) + grad_resid_norm
    grad_branch = grad_resid.astype(jnp.bfloat16)
    grad_out_weight = jnp.dot(merged.T, grad_branch, preferred_element_type=jnp.float32)
    grad_bias_out = jnp.sum(grad_branch.astype(jnp.float32), axis=0)
    grad_merged = jnp.dot(grad_branch, back_out.T, preferred_element_type=jnp.float32).astype(
        jnp.bfloat16
    )
    grad_head_result = lax.all_to_all(
        grad_merged.reshape(token_shape), "seq", split_axis=2, concat_axis=1, tiled=True
    )
    grad_q, grad_k, grad_v = lax.map(
        attend_backward, (head_q, head_k, head_v, valid, log_totals, grad_head_result)
    )
    tok_grad_q, tok_grad_k, tok_grad_v = (
        lax.all_to_all(grad_q, "seq", split_axis=1, concat_axis=2, tiled=True),
        lax.all_to_all(grad_k, "seq", split_axis=1, concat_axis=2, tiled=True),
        lax.all_to_all(grad_v, "seq", split_axis=1, concat_axis=2, tiled=True),
    )
    flat_grad_q = tok_grad_q.reshape(-1, model_width)
    flat_grad_v = tok_grad_v.reshape(-1, model_width)
    grad_mixed = jnp.concatenate(
        [flat_grad_q, tok_grad_k.reshape(-1, model_width), flat_grad_v], axis=1
    )
    grad_qkv = jnp.dot(first.T, grad_mixed, preferred_element_type=jnp.float32)
    grad_bias_q = jnp.sum(flat_grad_q.astype(jnp.float32), axis=0)
    grad_bias_v = jnp.sum(flat_grad_v.astype(jnp.float32), axis=0)
    grad_first = jnp.dot(grad_mixed, back_qkv.T, preferred_element_type=jnp.float32)
    grad_tok_norm, grad_gain_one, grad_bias_one = pull_one(grad_first)
    grad_tokens = (grad_resid + grad_tok_norm).reshape(token_shape)
    grad_gains = jnp.stack([grad_gain_one, grad_gain_two], axis=1)
    grad_biases = jnp.stack(
        [grad_bias_one, grad_bias_q, grad_bias_v, grad_bias_out, grad_bias_two, grad_bias_down],
        axis=1,
    )
    piece_qkv, piece_out, piece_up, piece_down, piece_gains, piece_biases, piece_upb = (
        lax.psum_scatter(
            grad_qkv.astype(jnp.bfloat16), "dp", scatter_dimension=0, tiled=True
        ).astype(jnp.float32),
        lax.psum_scatter(
            grad_out_weight.astype(jnp.bfloat16), "dp", scatter_dimension=0, tiled=True
        ).astype(jnp.float32),
        lax.psum_scatter(
            grad_up.astype(jnp.bfloat16), "dp", scatter_dimension=0, tiled=True
        ).astype(jnp.float32),
        lax.psum_scatter(
            grad_down.astype(jnp.bfloat16), "dp", scatter_dimension=0, tiled=True
        ).astype(jnp.float32),
        lax.psum_scatter(
            grad_gains.astype(jnp.bfloat16), "dp", scatter_dimension=0, tiled=True
        ).astype(jnp.float32),
        lax.psum_scatter(
            grad_biases.astype(jnp.bfloat16), "dp", scatter_dimension=0, tiled=True
        ).astype(jnp.float32),
        lax.psum_scatter(
            grad_up_bias.astype(jnp.bfloat16), "dp", scatter_dimension=0, tiled=True
        ).astype(jnp.float32),
    )
    totals = (
        lax.psum(piece_qkv.astype(jnp.bfloat16), "seq").astype(jnp.float32),
        lax.psum(piece_out.astype(jnp.bfloat16), "seq").astype(jnp.float32),
        lax.psum(piece_up.astype(jnp.bfloat16), "seq").astype(jnp.float32),
        lax.psum(piece_down.astype(jnp.bfloat16), "seq").astype(jnp.float32),
        lax.psum(piece_gains.astype(jnp.bfloat16), "seq").astype(jnp.float32),
        lax.psum(piece_biases.astype(jnp.bfloat16), "seq").astype(jnp.float32),
        lax.psum(piece_upb.astype(jnp.bfloat16), "seq").astype(jnp.float32),
    )
    return (
        out_tokens,
        grad_tokens,
        totals[0],
        totals[1],
        totals[2],
        totals[3],
        totals[4],
        totals[5],
        totals[6],
    )


def solution(mesh):
    return jax.shard_map(
        per_device,
        mesh=mesh,
        in_specs=(
            P("dp", "seq", None),
            P("dp", None),
            P("dp", None),
            P("dp", None),
            P("dp", None),
            P("dp", None),
            P("dp", None),
            P("dp"),
            P("dp"),
            P("dp", "seq", None),
        ),
        out_specs=(
            P("dp", "seq", None),
            P("dp", "seq", None),
            P("dp", None),
            P("dp", None),
            P("dp", None),
            P("dp", None),
            P("dp", None),
            P("dp", None),
            P("dp"),
        ),
        check_vma=False,
    )
```

profile of v0, /device:TPU:0, one launch (start us, length us, event | category | flops | bytes accessed | tf_op | source)
XLA Modules:
  0.0 1100.0 jit_solution(14046963542723650582)
XLA Ops:
  9.4 23.2 %all-gather = bf16[16,64,2]{1,2,0:T(2,128)(2,1)S(1)} all-gather(bf16[1,64,2]{1,2,0:T(2,128)(2,1)} %bitcast.251), channel_id=1, replica_groups=mesh['dp'=16,'seq'=2] {'dp'}, dimensions={0}, use_global_device_ids=true | all-gather | bytes 4352 | tf_op jit(solution)/shard_map/all_gather | solution.py:85
  32.7 17.9 %all-gather.1 = bf16[16,64,6]{1,2,0:T(8,128)(2,1)S(1)} all-gather(bf16[1,64,6]{1,2,0:T(8,128)(2,1)} %bitcast.250), channel_id=1, replica_groups=mesh['dp'=16,'seq'=2] {'dp'}, dimensions={0}, use_global_device_ids=true | all-gather | bytes 13056 | tf_op jit(solution)/shard_map/all_gather | solution.py:86
  53.4 21.5 %all-gather.8.cloned.1.call-done = bf16[1024,3072]{1,0:T(8,128)(2,1)} async-done(((bf16[64,3072]{1,0:T(8,128)(2,1)}), bf16[1024,3072]{1,0:T(8,128)(2,1)}) %all-gather.8.cloned.1.call-update) | async-done | bytes 6291472 | tf_op jit(solution)/shard_map/all_gather | solution.py:81
  208.8 16.1 %fusion.59 = (f32[8,1152]{1,0:T(8,128)S(1)}, f32[8,1152,1152]{1,2,0:T(8,128)}) fusion(bf16[1152,8,64]{0,2,1:T(8,128)(2,1)S(1)} %reshape.230, bf16[1152,8,64]{0,2,1:T(8,128)(2,1)S(1)} %reshape.232, pred[1152]{0:T(1024)(128)(4,1)S(1)} %iota_compare_fusion), kind=kOutput, calls=%fused_computation.104 | convolution fusion | flops 1390795776 | bytes 44864640 | tf_op jit(solution)/shard_map/while/body/eval_jaxpr/qhd,khd->hqk/dot_general | solution.py:28
  224.9 17.4 %fusion.1 = f32[8,1152]{1,0:T(8,128)S(1)} fusion(f32[8,1152,1152]{1,2,0:T(8,128)} %get-tuple-element.91, f32[8,1152]{1,0:T(8,128)S(1)} %get-tuple-element.90), kind=kLoop, calls=%fused_computation.7 | loop fusion | flops 21224448 | bytes 42541056 | tf_op jit(solution)/shard_map/while/body/eval_jaxpr/reduce_sum | solution.py:42
  242.4 18.1 %fusion.18 = bf16[8,64,1152]{2,1,0:T(8,128)(2,1)} fusion(bf16[1152,8,64]{0,2,1:T(8,128)(2,1)S(1)} %copy-done.17, f32[8,1152,1152]{1,2,0:T(8,128)} %get-tuple-element.91, f32[8,1152]{1,0:T(8,128)S(1)} %fusion.1, f32[8,1152]{1,0:T(8,128)S(1)} %get-tuple-element.90), kind=kOutput, calls=%fused_computation.39 | convolution fusion | flops 1391394816 | bytes 44900352 | tf_op jit(solution)/shard_map/while/body/eval_jaxpr/hqk,khd->qhd/dot_general | solution.py:44
  282.6 18.8 %all-gather.2 = bf16[16,1,256]{2,1,0:T(2,128)(2,1)S(1)} all-gather(bf16[1,1,256]{2,1,0:T(2,128)(2,1)S(1)} %reshape.246), channel_id=1, replica_groups=mesh['dp'=16,'seq'=2] {'dp'}, dimensions={0}, use_global_device_ids=true | all-gather | bytes 8704 | tf_op jit(solution)/shard_map/all_gather | solution.py:87
  310.8 30.8 %multiply_convert_fusion.1 = (bf16[576,4096]{1,0:T(8,128)(2,1)}, f32[576,4096]{1,0:T(8,128)}, f32[576,4096]{1,0:T(8,128)}) fusion(f32[4096]{0:T(1024)} %bitcast.240, bf16[1024,4096]{1,0:T(8,128)(2,1)} %all-gather.12.cloned.1.call-done, f32[576,1024]{1,0:T(8,128)S(1)} %get-tuple-element.93, f32[1024]{0:T(1024)} %bitcast.245, f32[1024]{0:T(1024)S(1)} %bitcast.234, ...), kind=kOutput, calls=%fused_computation.15 | convolution fusion | flops 4990500864 | bytes 34370048 | tf_op jit(solution)/shard_map/dot_general | solution.py:115
  341.7 15.7 %fusion.61 = (bf16[4096]{0:T(1024)(128)(2,1)}, bf16[576,4096]{1,0:T(8,128)(2,1)S(1)}) fusion(f32[576,4096]{1,0:T(8,128)} %get-tuple-element.79, bf16[4096,1024]{1,0:T(8,128)(2,1)} %all-gather.14.cloned.1.call-done, bf16[1,576,1024]{2,1,0:T(8,128)(2,1)S(1)} %copy-done.8, f32[576,4096]{1,0:T(8,128)} %get-tuple-element.94, f32[4096]{0:T(1024)} %bitcast.241), kind=kOutput, calls=%fused_computation.106 | convolution fusion | flops 4869582848 | bytes 33185792 | tf_op jit(solution)/shard_map/dot_general | solution.py:128
  357.4 10.7 multiply_reduce_fusion.1
  401.2 12.2 %all-to-all-done.4 = bf16[2,2,147456]{2,1,0:T(2,128)(2,1)} async-done(((bf16[2,2,147456]{2,1,0:T(2,128)(2,1)}), bf16[2,2,147456]{2,1,0:T(2,128)(2,1)}, u32[]{:S(2)}, u32[]{:S(2)}) %all-to-all-start.4) | async-done | bytes 1179680 | tf_op jit(solution)/shard_map/all_to_all | solution.py:141
  425.4 16.5 %fusion.15 = bf16[8,64,1152]{2,1,0:T(8,128)(2,1)S(1)} fusion(bf16[1152,8,64]{0,2,1:T(8,128)(2,1)S(1)} %reshape.237, f32[8,1152,1152]{1,2,0:T(8,128)} %get-tuple-element.91, f32[8,1152]{1,0:T(8,128)} %log_add_fusion), kind=kOutput, calls=%fused_computation.38 | convolution fusion | flops 1380777984 | bytes 44863488 | tf_op jit(solution)/shard_map/while/body/eval_jaxpr/hqk,qhd->khd/dot_general | solution.py:68
  442.0 32.1 %multiply_reduce_fusion = (f32[8,1152]{1,0:T(8,128)}, f32[8,1152,1152]{1,2,0:T(8,128)}) fusion(f32[8,1152,1152]{1,2,0:T(8,128)} %get-tuple-element.91, f32[8,1152]{1,0:T(8,128)} %log_add_fusion, bf16[1152,8,64]{0,2,1:T(8,128)(2,1)S(1)} %reshape.237, bf16[1152,8,64]{0,2,1:T(8,128)(2,1)S(1)} %copy-done.18), kind=kOutput, calls=%fused_computation.3 | convolution fusion | flops 1390795776 | bytes 87367680 | tf_op jit(solution)/shard_map/while/body/eval_jaxpr/qhd,khd->hqk/dot_general | solution.py:57
  492.1 34.8 %multiply_convert_fusion = bf16[8,1152,1152]{1,2,0:T(8,128)(2,1)} fusion(f32[8,1152,1152]{1,2,0:T(8,128)} %get-tuple-element.97, f32[8,1152,1152]{1,2,0:T(8,128)} %get-tuple-element.91, f32[8,1152]{1,0:T(8,128)S(1)} %copy-done.27, f32[8,1152]{1,0:T(8,128)S(1)} %copy-done.19), kind=kLoop, calls=%fused_computation.2 | loop fusion | flops 42467328 | bytes 106242048 | tf_op jit(solution)/shard_map/while/body/eval_jaxpr/convert_element_type | solution.py:61
  526.9 10.7 fusion.14
  555.7 10.5 fusion.13
  615.3 12.2 %convolution_convert_fusion = bf16[1024,4096]{1,0:T(8,128)(2,1)} fusion(bf16[576,4096]{1,0:T(8,128)(2,1)} %copy-done.49, f32[576,1024]{1,0:T(8,128)} %copy-done.10, f32[1024]{0:T(1024)} %bitcast.246, f32[1024]{0:T(1024)} %bitcast.237, f32[576]{0:T(1024)} %copy-done.40, f32[576]{0:T(1024)S(1)} %broadcast_multiply_fusion), kind=kOutput, calls=%fused_computation.29 | convolution fusion | flops 4838981632 | bytes 15479296 | tf_op jit(solution)/shard_map/dot_general | solution.py:130
  627.6 11.2 %convolution_convert_fusion.1 = bf16[4096,1024]{1,0:T(8,128)(2,1)} fusion(bf16[576,4096]{1,0:T(8,128)(2,1)} %get-tuple-element.78, bf16[1,576,1024]{2,1,0:T(8,128)(2,1)} %param.19), kind=kOutput, calls=%fused_computation.30 | convolution fusion | flops 4836032512 | bytes 14286848 | tf_op jit(solution)/shard_map/dot_general | solution.py:126
  664.7 31.7 %all-reduce = bf16[4096]{0:T(1024)(128)(2,1)S(1)} all-reduce(bf16[4096]{0:T(1024)(128)(2,1)} %get-tuple-element.99), channel_id=8, replica_groups=mesh['dp'=16,'seq'=2] {'dp'}, use_global_device_ids=true, to_apply=%region_32.33.clone | all-reduce | flops 4096 | bytes 16384
  698.9 107.8 %reduce-scatter.15.cloned.1.call-done = bf16[64,4096]{1,0:T(8,128)(2,1)} async-done(((bf16[1024,4096]{1,0:T(8,128)(2,1)}), bf16[64,4096]{1,0:T(8,128)(2,1)}) %reduce-scatter.15.cloned.1.call-update) | async-done | bytes 524304 | tf_op jit(solution)/shard_map/reduce_scatter | solution.py:175
  806.6 108.5 %reduce-scatter.17.cloned.1.call-done = bf16[256,1024]{1,0:T(8,128)(2,1)} async-done(((bf16[4096,1024]{1,0:T(8,128)(2,1)}), bf16[256,1024]{1,0:T(8,128)(2,1)}) %reduce-scatter.17.cloned.1.call-update) | async-done | bytes 524304 | tf_op jit(solution)/shard_map/reduce_scatter | solution.py:178
  927.9 46.4 %reduce-scatter.19.cloned.1.call-done = bf16[64,2]{1,0:T(8,128)(2,1)} async-done(((bf16[1024,2]{1,0:T(8,128)(2,1)}), bf16[64,2]{1,0:T(8,128)(2,1)}) %reduce-scatter.19.cloned.1.call-update) | async-done | bytes 272
  975.1 57.5 %reduce-scatter.21.cloned.1.call-done = bf16[64,6]{1,0:T(8,128)(2,1)} async-done(((bf16[1024,6]{1,0:T(8,128)(2,1)}), bf16[64,6]{1,0:T(8,128)(2,1)}) %reduce-scatter.21.cloned.1.call-update) | async-done | bytes 784
  1040.0 46.1 %all-reduce.5.cloned.1.call-done = (bf16[64,3072]{1,0:T(8,128)(2,1)}, bf16[64,1024]{1,0:T(8,128)(2,1)}, bf16[64,4096]{1,0:T(8,128)(2,1)}, bf16[256,1024]{1,0:T(8,128)(2,1)}) async-done(((bf16[64,3072]{1,0:T(8,128)(2,1)}, bf16[64,1024]{1,0:T(8,128)(2,1)}, bf16[64,4096]{1,0:T(8,128)(2,1)}, bf16[256,1024]{1,0:T(8,128)(2,1)}), (bf16[64,3072]{1,0:T(8,128)(2,1)}, bf16[64,1024]{1,0:T(8,128)(2,1)}, ...) | async-done | bytes 1572880 | tf_op jit(solution)/shard_map/psum | solution.py:192
  (267 shorter events, 355.1 us)
Async XLA Ops:
  7.2 45.0 %copy-start.2 = (bf16[1,576,1024]{2,1,0:T(8,128)(2,1)S(1)}, bf16[1,576,1024]{2,1,0:T(8,128)(2,1)}, u32[]{:S(2)}) copy-start(bf16[1,576,1024]{2,1,0:T(8,128)(2,1)} %param.10) | copy-start | bytes 3538948
  7.2 67.7 %all-gather.8.cloned.1.call-start = ((), (), s32[]{:S(2)}) async-start(), calls=%async_computation.14 | async-start | bytes 6684672 | tf_op jit(solution)/shard_map/all_gather | solution.py:81
  7.9 299.0 %all-gather.10.cloned.1.call-start = ((), (), s32[]{:S(2)}) async-start(), calls=%async_computation.15 | async-start | bytes 2228224 | tf_op jit(solution)/shard_map/all_gather | solution.py:82
  8.7 302.1 %all-gather.12.cloned.1.call-start = ((), (), s32[]{:S(2)}) async-start(), calls=%async_computation.16 | async-start | bytes 8912896 | tf_op jit(solution)/shard_map/all_gather | solution.py:83
  52.7 315.3 %copy-start.41 = (f32[1024,1]{0,1:T(1,128)}, f32[1024,1]{0,1:T(1,128)S(1)}, u32[]{:S(2)}) copy-start(f32[1024,1]{0,1:T(1,128)S(1)} %get-tuple-element.88) | copy-start | bytes 12292
  101.3 23.0 %all-to-all-start.1 = ((bf16[2,2,147456]{2,1,0:T(2,128)(2,1)}), bf16[2,2,147456]{2,1,0:T(2,128)(2,1)}, u32[]{:S(2)}, u32[]{:S(2)}) async-start(bf16[2,2,147456]{2,1,0:T(2,128)(2,1)} %reshape.262), calls=%async_computation.1 | async-start | bytes 2359296 | tf_op jit(solution)/shard_map/all_to_all | solution.py:102
  124.3 21.5 %all-to-all-start.2 = ((bf16[2,2,147456]{2,1,0:T(2,128)(2,1)}), bf16[2,2,147456]{2,1,0:T(2,128)(2,1)}, u32[]{:S(2)}, u32[]{:S(2)}) async-start(bf16[2,2,147456]{2,1,0:T(2,128)(2,1)} %reshape.264), calls=%async_computation.2 | async-start | bytes 2359296 | tf_op jit(solution)/shard_map/all_to_all | solution.py:105
  145.8 41.7 %all-to-all-start = ((bf16[2,2,147456]{2,1,0:T(2,128)(2,1)}), bf16[2,2,147456]{2,1,0:T(2,128)(2,1)}, u32[]{:S(2)}, u32[]{:S(2)}) async-start(bf16[2,2,147456]{2,1,0:T(2,128)(2,1)} %reshape.260), calls=%async_computation | async-start | bytes 2359296 | tf_op jit(solution)/shard_map/all_to_all | solution.py:106
  150.3 191.4 %all-gather.14.cloned.1.call-start = ((), (), s32[]{:S(2)}) async-start(), calls=%async_computation.17 | async-start | bytes 8912896 | tf_op jit(solution)/shard_map/all_gather | solution.py:84
  278.1 23.9 %all-to-all-start.3 = ((bf16[2,2,147456]{2,1,0:T(2,128)(2,1)}), bf16[2,2,147456]{2,1,0:T(2,128)(2,1)}, u32[]{:S(2)}, u32[]{:S(2)}) async-start(bf16[2,2,147456]{2,1,0:T(2,128)(2,1)} %reshape.266), calls=%async_computation.3 | async-start | bytes 2359296 | tf_op jit(solution)/shard_map/all_to_all | solution.py:109
  310.4 57.7 %copy-start.10 = (f32[576,1024]{1,0:T(8,128)}, f32[576,1024]{1,0:T(8,128)S(1)}, u32[]{:S(2)}) copy-start(f32[576,1024]{1,0:T(8,128)S(1)} %get-tuple-element.93) | copy-start | bytes 7077892
  310.8 57.3 %copy-start.40 = (f32[576]{0:T(1024)}, f32[576]{0:T(1024)S(1)}, u32[]{:S(2)}) copy-start(f32[576]{0:T(1024)S(1)} %fusion.46) | copy-start | bytes 6916
  392.8 20.6 %all-to-all-start.4 = ((bf16[2,2,147456]{2,1,0:T(2,128)(2,1)}), bf16[2,2,147456]{2,1,0:T(2,128)(2,1)}, u32[]{:S(2)}, u32[]{:S(2)}) async-start(bf16[2,2,147456]{2,1,0:T(2,128)(2,1)} %reshape.268), calls=%async_computation.4 | async-start | bytes 2359296 | tf_op jit(solution)/shard_map/all_to_all | solution.py:141
  397.3 299.1 %reduce-scatter.13.cloned.1.call-start = ((), (), s32[]{:S(2)}) async-start(), calls=%async_computation.19 | async-start | bytes 2228224 | tf_op jit(solution)/shard_map/reduce_scatter | solution.py:172
  487.6 63.7 %all-to-all-start.7 = ((bf16[2,2,147456]{2,1,0:T(2,128)(2,1)}), bf16[2,2,147456]{2,1,0:T(2,128)(2,1)}, u32[]{:S(2)}, u32[]{:S(2)}) async-start(bf16[2,2,147456]{2,1,0:T(2,128)(2,1)} %reshape.274), calls=%async_computation.7 | async-start | bytes 2359296 | tf_op jit(solution)/shard_map/all_to_all | solution.py:150
  551.2 28.5 %all-to-all-start.6 = ((bf16[2,2,147456]{2,1,0:T(2,128)(2,1)}), bf16[2,2,147456]{2,1,0:T(2,128)(2,1)}, u32[]{:S(2)}, u32[]{:S(2)}) async-start(bf16[2,2,147456]{2,1,0:T(2,128)(2,1)} %reshape.272), calls=%async_computation.6 | async-start | bytes 2359296 | tf_op jit(solution)/shard_map/all_to_all | solution.py:149
  579.8 19.1 %all-to-all-start.5 = ((bf16[2,2,147456]{2,1,0:T(2,128)(2,1)}), bf16[2,2,147456]{2,1,0:T(2,128)(2,1)S(1)}, u32[]{:S(2)}, u32[]{:S(2)}) async-start(bf16[2,2,147456]{2,1,0:T(2,128)(2,1)} %reshape.270), calls=%async_computation.5 | async-start | bytes 2359296 | tf_op jit(solution)/shard_map/all_to_all | solution.py:148
  583.4 115.5 %reduce-scatter.11.cloned.1.call-start = ((), (), s32[]{:S(2)}) async-start(), calls=%async_computation.18 | async-start | bytes 6684672 | tf_op jit(solution)/shard_map/reduce_scatter | solution.py:169
  615.3 191.4 %reduce-scatter.15.cloned.1.call-start = ((), (), s32[]{:S(2)}) async-start(), calls=%async_computation.20 | async-start | bytes 8912896 | tf_op jit(solution)/shard_map/reduce_scatter | solution.py:175
  627.5 287.6 %reduce-scatter.17.cloned.1.call-start = ((), (), s32[]{:S(2)}) async-start(), calls=%async_computation.21 | async-start | bytes 8912896 | tf_op jit(solution)/shard_map/reduce_scatter | solution.py:178
  638.8 335.5 %reduce-scatter.19.cloned.1.call-start = ((), (), s32[]{:S(2)}) async-start(), calls=%async_computation.22 | async-start | bytes 278528
  652.7 379.9 %reduce-scatter.21.cloned.1.call-start = ((), (), s32[]{:S(2)}) async-start(), calls=%async_computation.23 | async-start | bytes 278528
  659.5 255.7 %copy-start.43 = (f32[1024,1]{0,1:T(1,128)S(1)}, f32[1024,1]{0,1:T(1,128)}, u32[]{:S(2)}) copy-start(f32[1024,1]{0,1:T(1,128)} %get-tuple-element.82) | copy-start | bytes 12292
  662.7 423.5 %all-reduce.5.cloned.1.call-start = ((), (), s32[]{:S(2)}) async-start(), calls=%async_computation.24 | async-start | bytes 3145728 | tf_op jit(solution)/shard_map/psum | solution.py:192
  (45 other events, 507.2 us)
Sparse Core Ops, SparseCore 0:
  10.3 64.5 all-gather.7
  77.1 40.0 all-gather.9
  119.4 73.6 all-gather.11
  195.1 73.1 all-gather.13
  401.6 59.3 reduce-scatter.12
  615.4 83.4 reduce-scatter.10
  702.9 103.6 reduce-scatter.14
  810.7 104.3 reduce-scatter.16
  919.2 55.0 reduce-scatter.18
  978.2 54.3 reduce-scatter.20
  1035.1 51.0 all-reduce.4
where the time goes:
time: 1110 us; the launch traced here: 1100 us
  waiting for transfers between devices  405 us (36%)
  matrix products  226 us (20%)
  local copies, waits for them, and re-layouts  173 us (16%)
  other arithmetic  147 us (13%)
  blocking collectives  96.4 us (9%)
  starting transfers between devices  35.5 us (3%)
  between operations  16.6 us (1%)
    reduce_scatter x1, waiting for transfers between devices, per_device(): lax.psum_scatter(grad_down.astype(jnp.bfloat16), 'dp', scatter_dimension=...  108 us
    reduce_scatter x1, waiting for transfers between devices, per_device(): lax.psum_scatter(grad_up.astype(jnp.bfloat16), 'dp', scatter_dimension=0,...  108 us
    unnamed x13, waiting for transfers between devices  107 us
    unnamed x140, local copies, waits for them, and re-layouts  80.5 us
    unnamed x8, other arithmetic  71.4 us
    psum x1, waiting for transfers between devices, per_device(): lax.psum(piece_qkv.astype(jnp.bfloat16), 'seq').astype(jnp.float32)  46.1 us
    convert_element_type x1, other arithmetic, attend_backward(): grad_scores = (probs * (grad_probs - row_delta)).astype(jnp.bfloat16)  34.8 us
    dot_general x1, matrix products, attend_backward(): jnp.einsum('qhd,khd->hqk', grad_heads, value_heads, preferred_element_typ...  32.1 us
  transfers between devices with their start and end apart: 19, of which 8 were waited for; matrix products, arithmetic and copies ran while one was open for 44% of the time, Pallas kernels for 0%

commit v1 on v0

--- a/solution.py
+++ b/solution.py
@@ -6,6 +6,19 @@
 HD = 64
 EPSILON = 1e-06
 NEG_FILL = -1e30
+
+
+def ring_gather(x, axis, dim):
+    ways = lax.axis_size(axis)
+    up = [(d, (d + 1) % ways) for d in range(ways)]
+    down = [(d, (d - 1) % ways) for d in range(ways)]
+    earlier, later = ([x], [x])
+    for _ in range(ways // 2):
+        earlier.append(lax.ppermute(earlier[-1], axis, up))
+    for _ in range((ways - 1) // 2):
+        later.append(lax.ppermute(later[-1], axis, down))
+    line = jnp.concatenate([*earlier[::-1], *later[1:]], axis=dim)
+    return jnp.roll(line, (lax.axis_index(axis) - ways // 2) * x.shape[dim], axis=dim)
 
 
 def layer_norm(values, scales, offset):
@@ -82,7 +95,7 @@
         lax.all_gather(w_out, "dp", axis=0, tiled=True),
         lax.all_gather(w_up, "dp", axis=0, tiled=True),
         lax.all_gather(w_down, "dp", axis=0, tiled=True),
-        lax.all_gather(gains, "dp", axis=0, tiled=True),
+        ring_gather(gains, "dp", 0),
         lax.all_gather(biases, "dp", axis=0, tiled=True),
         lax.all_gather(up_bias, "dp", axis=0, tiled=True),
     )

time: 1110 us -> 1110 us (level)
  starting transfers between devices: 35.5 us -> 68.8 us
  blocking collectives: 96.4 us -> 74.8 us
    ppermute x0 -> x15, starting transfers between devices: none -> 32.4 us  [the longest x7 31.3 us: ring_gather(): later.append(lax.ppermute(later[-1], axis, down))]
    all_gather x1 -> x0, blocking collectives: 23.2 us -> none  [per_device(): lax.all_gather(gains, 'dp', axis=0, tiled=True)]
    all_gather x1, waiting for transfers between devices: 21.5 us -> 0.02 us  [per_device(): lax.all_gather(w_qkv, 'dp', axis=0, tiled=True)]
    ppermute x0 -> x15, waiting for transfers between devices: none -> 13.4 us  [the longest x8 13.2 us: ring_gather(): earlier.append(lax.ppermute(earlier[-1], axis, up))]
    unnamed x140 -> x142, local copies, waits for them, and re-layouts: 80.5 us -> 80.4 us
  transfers between devices with their start and end apart: 19 -> 34, of which waited for: 8 -> 15; matrix products, arithmetic and copies ran while one was open for 44% -> 44% of each run, Pallas kernels for 0% -> 0%
where the time goes in v1:
time: 1110 us; the launch traced here: 1100 us
  waiting for transfers between devices  397 us (36%)
  matrix products  226 us (20%)
  local copies, waits for them, and re-layouts  173 us (16%)
  other arithmetic  147 us (13%)
  blocking collectives  74.8 us (7%)
  starting transfers between devices  68.8 us (6%)
  between operations  16.6 us (1%)
    reduce_scatter x1, waiting for transfers between devices, per_device(): lax.psum_scatter(grad_down.astype(jnp.bfloat16), 'dp', scatter_dimension=...  108 us
    reduce_scatter x1, waiting for transfers between devices, per_device(): lax.psum_scatter(grad_up.astype(jnp.bfloat16), 'dp', scatter_dimension=0,...  108 us
    unnamed x13, waiting for transfers between devices  106 us
    unnamed x142, local copies, waits for them, and re-layouts  80.4 us
    unnamed x8, other arithmetic  71.5 us
    psum x1, waiting for transfers between devices, per_device(): lax.psum(piece_qkv.astype(jnp.bfloat16), 'seq').astype(jnp.float32)  46.1 us
    convert_element_type x1, other arithmetic, attend_backward(): grad_scores = (probs * (grad_probs - row_delta)).astype(jnp.bfloat16)  34.7 us
    unnamed x1, blocking collectives  33 us
  transfers between devices with their start and end apart: 34, of which 15 were waited for; matrix products, arithmetic and copies ran while one was open for 44% of the time, Pallas kernels for 0%

profile of v1, /device:TPU:0, one launch (start us, length us, event | category | flops | bytes accessed | tf_op | source)
XLA Modules:
  0.0 1102.7 jit_solution(7542160958769585204)
XLA Ops:
  15.0 19.8 %all-gather = bf16[16,64,6]{1,2,0:T(8,128)(2,1)S(1)} all-gather(bf16[1,64,6]{1,2,0:T(8,128)(2,1)} %bitcast.247), channel_id=1, replica_groups=mesh['dp'=16,'seq'=2] {'dp'}, dimensions={0}, use_global_device_ids=true | all-gather | bytes 13056 | tf_op jit(solution)/shard_map/all_gather | solution.py:99
  212.0 16.8 %fusion.59 = (f32[8,1152]{1,0:T(8,128)S(1)}, f32[8,1152,1152]{1,2,0:T(8,128)}) fusion(bf16[1152,8,64]{0,2,1:T(8,128)(2,1)S(1)} %reshape.230, bf16[1152,8,64]{0,2,1:T(8,128)(2,1)S(1)} %reshape.232, pred[1152]{0:T(1024)(128)(4,1)S(1)} %iota_compare_fusion), kind=kOutput, calls=%fused_computation.104 | convolution fusion | flops 1390795776 | bytes 44864640 | tf_op jit(solution)/shard_map/while/body/eval_jaxpr/qhd,khd->hqk/dot_general | solution.py:41
  228.8 16.6 %fusion.1 = f32[8,1152]{1,0:T(8,128)S(1)} fusion(f32[8,1152,1152]{1,2,0:T(8,128)} %get-tuple-element.91, f32[8,1152]{1,0:T(8,128)S(1)} %get-tuple-element.90), kind=kLoop, calls=%fused_computation.7 | loop fusion | flops 21224448 | bytes 42541056 | tf_op jit(solution)/shard_map/while/body/eval_jaxpr/reduce_sum | solution.py:55
  245.4 18.1 %fusion.18 = bf16[8,64,1152]{2,1,0:T(8,128)(2,1)} fusion(bf16[1152,8,64]{0,2,1:T(8,128)(2,1)S(1)} %copy-done.17, f32[8,1152,1152]{1,2,0:T(8,128)} %get-tuple-element.91, f32[8,1152]{1,0:T(8,128)S(1)} %fusion.1, f32[8,1152]{1,0:T(8,128)S(1)} %get-tuple-element.90), kind=kOutput, calls=%fused_computation.39 | convolution fusion | flops 1391394816 | bytes 44900352 | tf_op jit(solution)/shard_map/while/body/eval_jaxpr/hqk,khd->qhd/dot_general | solution.py:57
  285.6 17.1 %all-gather.1 = bf16[16,1,256]{2,1,0:T(2,128)(2,1)S(1)} all-gather(bf16[1,1,256]{2,1,0:T(2,128)(2,1)S(1)} %reshape.244), channel_id=1, replica_groups=mesh['dp'=16,'seq'=2] {'dp'}, dimensions={0}, use_global_device_ids=true | all-gather | bytes 8704 | tf_op jit(solution)/shard_map/all_gather | solution.py:100
  312.3 30.8 %multiply_convert_fusion.1 = (bf16[576,4096]{1,0:T(8,128)(2,1)}, f32[576,4096]{1,0:T(8,128)}, f32[576,4096]{1,0:T(8,128)}) fusion(f32[4096]{0:T(1024)} %bitcast.237, bf16[1024,4096]{1,0:T(8,128)(2,1)} %all-gather.11.cloned.1.call-done, f32[576,1024]{1,0:T(8,128)S(1)} %get-tuple-element.93, f32[1024]{0:T(1024)} %bitcast.242, f32[1024]{0:T(1024)S(1)} %bitcast.231, ...), kind=kOutput, calls=%fused_computation.15 | convolution fusion | flops 4990500864 | bytes 34370048 | tf_op jit(solution)/shard_map/dot_general | solution.py:128
  343.1 15.7 %fusion.61 = (bf16[4096]{0:T(1024)(128)(2,1)}, bf16[576,4096]{1,0:T(8,128)(2,1)S(1)}) fusion(f32[576,4096]{1,0:T(8,128)} %get-tuple-element.79, bf16[4096,1024]{1,0:T(8,128)(2,1)} %all-gather.13.cloned.1.call-done, bf16[1,576,1024]{2,1,0:T(8,128)(2,1)S(1)} %copy-done.8, f32[576,4096]{1,0:T(8,128)} %get-tuple-element.94, f32[4096]{0:T(1024)} %bitcast.238), kind=kOutput, calls=%fused_computation.106 | convolution fusion | flops 4869582848 | bytes 33185792 | tf_op jit(solution)/shard_map/dot_general | solution.py:141
  358.8 10.7 multiply_reduce_fusion.1
  380.6 10.1 reduce.14
  402.8 12.2 %all-to-all-done.4 = bf16[2,2,147456]{2,1,0:T(2,128)(2,1)} async-done(((bf16[2,2,147456]{2,1,0:T(2,128)(2,1)}), bf16[2,2,147456]{2,1,0:T(2,128)(2,1)}, u32[]{:S(2)}, u32[]{:S(2)}) %all-to-all-start.4) | async-done | bytes 1179680 | tf_op jit(solution)/shard_map/all_to_all | solution.py:154
  427.0 16.5 %fusion.15 = bf16[8,64,1152]{2,1,0:T(8,128)(2,1)S(1)} fusion(bf16[1152,8,64]{0,2,1:T(8,128)(2,1)S(1)} %reshape.237, f32[8,1152,1152]{1,2,0:T(8,128)} %get-tuple-element.91, f32[8,1152]{1,0:T(8,128)} %log_add_fusion), kind=kOutput, calls=%fused_computation.38 | convolution fusion | flops 1380777984 | bytes 44863488 | tf_op jit(solution)/shard_map/while/body/eval_jaxpr/hqk,qhd->khd/dot_general | solution.py:81
  443.5 32.0 %multiply_reduce_fusion = (f32[8,1152]{1,0:T(8,128)}, f32[8,1152,1152]{1,2,0:T(8,128)}) fusion(f32[8,1152,1152]{1,2,0:T(8,128)} %get-tuple-element.91, f32[8,1152]{1,0:T(8,128)} %log_add_fusion, bf16[1152,8,64]{0,2,1:T(8,128)(2,1)S(1)} %reshape.237, bf16[1152,8,64]{0,2,1:T(8,128)(2,1)S(1)} %copy-done.18), kind=kOutput, calls=%fused_computation.3 | convolution fusion | flops 1390795776 | bytes 87367680 | tf_op jit(solution)/shard_map/while/body/eval_jaxpr/qhd,khd->hqk/dot_general | solution.py:70
  493.6 34.7 %multiply_convert_fusion = bf16[8,1152,1152]{1,2,0:T(8,128)(2,1)} fusion(f32[8,1152,1152]{1,2,0:T(8,128)} %get-tuple-element.97, f32[8,1152,1152]{1,2,0:T(8,128)} %get-tuple-element.91, f32[8,1152]{1,0:T(8,128)S(1)} %copy-done.27, f32[8,1152]{1,0:T(8,128)S(1)} %copy-done.19), kind=kLoop, calls=%fused_computation.2 | loop fusion | flops 42467328 | bytes 106242048 | tf_op jit(solution)/shard_map/while/body/eval_jaxpr/convert_element_type | solution.py:74
  528.3 10.7 fusion.14
  557.1 10.5 fusion.13
  616.6 12.2 %convolution_convert_fusion = bf16[1024,4096]{1,0:T(8,128)(2,1)} fusion(bf16[576,4096]{1,0:T(8,128)(2,1)} %copy-done.50, f32[576,1024]{1,0:T(8,128)} %copy-done.10, f32[1024]{0:T(1024)} %bitcast.243, f32[1024]{0:T(1024)} %bitcast.234, f32[576]{0:T(1024)} %copy-done.40, f32[576]{0:T(1024)S(1)} %broadcast_multiply_fusion), kind=kOutput, calls=%fused_computation.29 | convolution fusion | flops 4838981632 | bytes 15479296 | tf_op jit(solution)/shard_map/dot_general | solution.py:143
  628.9 11.1 %convolution_convert_fusion.1 = bf16[4096,1024]{1,0:T(8,128)(2,1)} fusion(bf16[576,4096]{1,0:T(8,128)(2,1)} %get-tuple-element.78, bf16[1,576,1024]{2,1,0:T(8,128)(2,1)} %param.19), kind=kOutput, calls=%fused_computation.30 | convolution fusion | flops 4836032512 | bytes 14286848 | tf_op jit(solution)/shard_map/dot_general | solution.py:139
  665.9 33.0 %all-reduce = bf16[4096]{0:T(1024)(128)(2,1)S(1)} all-reduce(bf16[4096]{0:T(1024)(128)(2,1)} %get-tuple-element.99), channel_id=8, replica_groups=mesh['dp'=16,'seq'=2] {'dp'}, use_global_device_ids=true, to_apply=%region_32.33.clone | all-reduce | flops 4096 | bytes 16384
  701.5 108.0 %reduce-scatter.15.cloned.1.call-done = bf16[64,4096]{1,0:T(8,128)(2,1)} async-done(((bf16[1024,4096]{1,0:T(8,128)(2,1)}), bf16[64,4096]{1,0:T(8,128)(2,1)}) %reduce-scatter.15.cloned.1.call-update) | async-done | bytes 524304 | tf_op jit(solution)/shard_map/reduce_scatter | solution.py:188
  809.5 108.4 %reduce-scatter.17.cloned.1.call-done = bf16[256,1024]{1,0:T(8,128)(2,1)} async-done(((bf16[4096,1024]{1,0:T(8,128)(2,1)}), bf16[256,1024]{1,0:T(8,128)(2,1)}) %reduce-scatter.17.cloned.1.call-update) | async-done | bytes 524304 | tf_op jit(solution)/shard_map/reduce_scatter | solution.py:191
  918.0 10.5 fusion.36
  930.7 46.4 %reduce-scatter.19.cloned.1.call-done = bf16[64,2]{1,0:T(8,128)(2,1)} async-done(((bf16[1024,2]{1,0:T(8,128)(2,1)}), bf16[64,2]{1,0:T(8,128)(2,1)}) %reduce-scatter.19.cloned.1.call-update) | async-done | bytes 272
  977.9 57.5 %reduce-scatter.21.cloned.1.call-done = bf16[64,6]{1,0:T(8,128)(2,1)} async-done(((bf16[1024,6]{1,0:T(8,128)(2,1)}), bf16[64,6]{1,0:T(8,128)(2,1)}) %reduce-scatter.21.cloned.1.call-update) | async-done | bytes 784
  1042.8 46.1 %all-reduce.5.cloned.1.call-done = (bf16[64,3072]{1,0:T(8,128)(2,1)}, bf16[64,1024]{1,0:T(8,128)(2,1)}, bf16[64,4096]{1,0:T(8,128)(2,1)}, bf16[256,1024]{1,0:T(8,128)(2,1)}) async-done(((bf16[64,3072]{1,0:T(8,128)(2,1)}, bf16[64,1024]{1,0:T(8,128)(2,1)}, bf16[64,4096]{1,0:T(8,128)(2,1)}, bf16[256,1024]{1,0:T(8,128)(2,1)}), (bf16[64,3072]{1,0:T(8,128)(2,1)}, bf16[64,1024]{1,0:T(8,128)(2,1)}, ...) | async-done | bytes 1572880 | tf_op jit(solution)/shard_map/psum | solution.py:205
  (298 shorter events, 380.6 us)
Async XLA Ops:
  7.2 70.7 %all-gather.7.cloned.1.call-start = ((), (), s32[]{:S(2)}) async-start(), calls=%async_computation.14 | async-start | bytes 6684672 | tf_op jit(solution)/shard_map/all_gather | solution.py:94
  7.9 300.4 %all-gather.9.cloned.1.call-start = ((), (), s32[]{:S(2)}) async-start(), calls=%async_computation.15 | async-start | bytes 2228224 | tf_op jit(solution)/shard_map/all_gather | solution.py:95
  8.7 303.6 %all-gather.11.cloned.1.call-start = ((), (), s32[]{:S(2)}) async-start(), calls=%async_computation.16 | async-start | bytes 8912896 | tf_op jit(solution)/shard_map/all_gather | solution.py:96
  9.4 28.0 %collective-permute-start = (bf16[64,2]{0,1:T(2,128)(2,1)}, bf16[64,2]{0,1:T(2,128)(2,1)S(1)}, u32[]{:S(2)}, u32[]{:S(2)}) collective-permute-start(bf16[64,2]{0,1:T(2,128)(2,1)} %param.15), channel_id=1, source_target_pairs={{0,2},{2,4},{4,6},{6,8},{8,10},{10,12},{12,14},{14,16},{16,18},{18... | collective-permute-start | bytes 776 | tf_op jit(solution)/shard_map/ppermute | solution.py:17
  9.9 27.9 %collective-permute-start.8 = (bf16[64,2]{0,1:T(2,128)(2,1)}, bf16[64,2]{0,1:T(2,128)(2,1)S(1)}, u32[]{:S(2)}, u32[]{:S(2)}) collective-permute-start(bf16[64,2]{0,1:T(2,128)(2,1)} %param.15), channel_id=1, source_target_pairs={{0,30},{2,0},{4,2},{6,4},{8,6},{10,8},{12,10},{14,12},{16,14},{18,... | collective-permute-start | bytes 776 | tf_op jit(solution)/shard_map/ppermute | solution.py:19
  43.1 5.8 collective-permute-start.2
  66.2 5.9 collective-permute-start.14
  71.8 5.9 collective-permute-start.7
  104.3 23.1 %all-to-all-start.1 = ((bf16[2,2,147456]{2,1,0:T(2,128)(2,1)}), bf16[2,2,147456]{2,1,0:T(2,128)(2,1)}, u32[]{:S(2)}, u32[]{:S(2)}) async-start(bf16[2,2,147456]{2,1,0:T(2,128)(2,1)} %reshape.259), calls=%async_computation.1 | async-start | bytes 2359296 | tf_op jit(solution)/shard_map/all_to_all | solution.py:115
  127.4 21.6 %all-to-all-start.2 = ((bf16[2,2,147456]{2,1,0:T(2,128)(2,1)}), bf16[2,2,147456]{2,1,0:T(2,128)(2,1)}, u32[]{:S(2)}, u32[]{:S(2)}) async-start(bf16[2,2,147456]{2,1,0:T(2,128)(2,1)} %reshape.261), calls=%async_computation.2 | async-start | bytes 2359296 | tf_op jit(solution)/shard_map/all_to_all | solution.py:118
  149.0 41.7 %all-to-all-start = ((bf16[2,2,147456]{2,1,0:T(2,128)(2,1)}), bf16[2,2,147456]{2,1,0:T(2,128)(2,1)}, u32[]{:S(2)}, u32[]{:S(2)}) async-start(bf16[2,2,147456]{2,1,0:T(2,128)(2,1)} %reshape.257), calls=%async_computation | async-start | bytes 2359296 | tf_op jit(solution)/shard_map/all_to_all | solution.py:119
  153.6 189.6 %all-gather.13.cloned.1.call-start = ((), (), s32[]{:S(2)}) async-start(), calls=%async_computation.17 | async-start | bytes 8912896 | tf_op jit(solution)/shard_map/all_gather | solution.py:97
  281.2 22.2 %all-to-all-start.3 = ((bf16[2,2,147456]{2,1,0:T(2,128)(2,1)}), bf16[2,2,147456]{2,1,0:T(2,128)(2,1)}, u32[]{:S(2)}, u32[]{:S(2)}) async-start(bf16[2,2,147456]{2,1,0:T(2,128)(2,1)} %reshape.263), calls=%async_computation.3 | async-start | bytes 2359296 | tf_op jit(solution)/shard_map/all_to_all | solution.py:122
  394.4 20.6 %all-to-all-start.4 = ((bf16[2,2,147456]{2,1,0:T(2,128)(2,1)}), bf16[2,2,147456]{2,1,0:T(2,128)(2,1)}, u32[]{:S(2)}, u32[]{:S(2)}) async-start(bf16[2,2,147456]{2,1,0:T(2,128)(2,1)} %reshape.265), calls=%async_computation.4 | async-start | bytes 2359296 | tf_op jit(solution)/shard_map/all_to_all | solution.py:154
  398.8 300.1 %reduce-scatter.13.cloned.1.call-start = ((), (), s32[]{:S(2)}) async-start(), calls=%async_computation.19 | async-start | bytes 2228224 | tf_op jit(solution)/shard_map/reduce_scatter | solution.py:185
  489.1 63.6 %all-to-all-start.7 = ((bf16[2,2,147456]{2,1,0:T(2,128)(2,1)}), bf16[2,2,147456]{2,1,0:T(2,128)(2,1)}, u32[]{:S(2)}, u32[]{:S(2)}) async-start(bf16[2,2,147456]{2,1,0:T(2,128)(2,1)} %reshape.271), calls=%async_computation.7 | async-start | bytes 2359296 | tf_op jit(solution)/shard_map/all_to_all | solution.py:163
  552.6 28.6 %all-to-all-start.6 = ((bf16[2,2,147456]{2,1,0:T(2,128)(2,1)}), bf16[2,2,147456]{2,1,0:T(2,128)(2,1)}, u32[]{:S(2)}, u32[]{:S(2)}) async-start(bf16[2,2,147456]{2,1,0:T(2,128)(2,1)} %reshape.269), calls=%async_computation.6 | async-start | bytes 2359296 | tf_op jit(solution)/shard_map/all_to_all | solution.py:162
  581.2 19.1 %all-to-all-start.5 = ((bf16[2,2,147456]{2,1,0:T(2,128)(2,1)}), bf16[2,2,147456]{2,1,0:T(2,128)(2,1)S(1)}, u32[]{:S(2)}, u32[]{:S(2)}) async-start(bf16[2,2,147456]{2,1,0:T(2,128)(2,1)} %reshape.267), calls=%async_computation.5 | async-start | bytes 2359296 | tf_op jit(solution)/shard_map/all_to_all | solution.py:161
  584.8 116.7 %reduce-scatter.11.cloned.1.call-start = ((), (), s32[]{:S(2)}) async-start(), calls=%async_computation.18 | async-start | bytes 6684672 | tf_op jit(solution)/shard_map/reduce_scatter | solution.py:182
  616.6 192.9 %reduce-scatter.15.cloned.1.call-start = ((), (), s32[]{:S(2)}) async-start(), calls=%async_computation.20 | async-start | bytes 8912896 | tf_op jit(solution)/shard_map/reduce_scatter | solution.py:188
  628.8 289.0 %reduce-scatter.17.cloned.1.call-start = ((), (), s32[]{:S(2)}) async-start(), calls=%async_computation.21 | async-start | bytes 8912896 | tf_op jit(solution)/shard_map/reduce_scatter | solution.py:191
  640.1 337.0 %reduce-scatter.19.cloned.1.call-start = ((), (), s32[]{:S(2)}) async-start(), calls=%async_computation.22 | async-start | bytes 278528
  654.0 381.3 %reduce-scatter.21.cloned.1.call-start = ((), (), s32[]{:S(2)}) async-start(), calls=%async_computation.23 | async-start | bytes 278528
  664.0 425.0 %all-reduce.5.cloned.1.call-start = ((), (), s32[]{:S(2)}) async-start(), calls=%async_computation.24 | async-start | bytes 3145728 | tf_op jit(solution)/shard_map/psum | solution.py:205
  (61 other events, 1380.0 us)
Sparse Core Ops, SparseCore 0:
  10.3 64.5 all-gather.6
  77.0 40.0 all-gather.8
  119.3 73.6 all-gather.10
  195.0 73.1 all-gather.12
  403.1 60.7 reduce-scatter.12
  616.7 84.7 reduce-scatter.10
  705.6 103.8 reduce-scatter.14
  813.5 104.3 reduce-scatter.16
  922.0 55.0 reduce-scatter.18
  981.0 54.2 reduce-scatter.20
  1037.8 51.0 all-reduce.4
